TPU v7x, 512 devices: a whole 4x4x16 slice. The times are simulated.
512 devices in a mesh: leaf: 32 (over x, z_lo, core), col: 16 (over y, z_hi).
Axes of the slice: x: 4, y: 4, z: 16 (z_hi: 4, z_lo: 4; z = z_hi * 4 + z_lo), core: 2. Of those that a mesh axis runs over, the one named last changes fastest.
Arguments:
- right_sides: float32 [256, 65536], P('col', 'leaf'), may hold values from -6 to 6
- inverse_first: float32 [128, 128, 128], P('leaf'), may hold values from -0.5 to 0.5
- coupling_first: float32 [128, 3, 128, 128], P('leaf'), may hold values from -0.3125 to 0.3125
- links_first: int32 [128, 3], P('leaf'), may hold values from 0 to 11, as said below
- order_first: int32 [32, 12], P('leaf'), may hold values from 0 to 11, as said below
- inverse_second: float32 [128, 128, 128], P('leaf'), may hold values from -0.5 to 0.5
- coupling_second: float32 [128, 3, 128, 128], P('leaf'), may hold values from -0.3125 to 0.3125
- links_second: int32 [128, 3], P('leaf'), may hold values from 0 to 7, as said below
- order_second: int32 [32, 8], P('leaf'), may hold values from 0 to 7, as said below
- inverse_third: float32 [128, 128, 128], P('leaf'), may hold values from -0.5 to 0.5
- coupling_third: float32 [128, 3, 128, 128], P('leaf'), may hold values from -0.3125 to 0.3125
- links_third: int32 [128, 3], P('leaf'), may hold values from 0 to 3, as said below
- order_third: int32 [32, 4], P('leaf'), may hold values from 0 to 3, as said below
- front_rows: int32 [3, 32], P(None, 'leaf'), may hold values from 128 to 512
- root_inverse: float32 [2, 8192, 8192], P(None, 'leaf', 'col'), may hold values from -0.0625 to 0.0625
- root_coupling: float32 [8192, 8192], P('leaf', 'col'), may hold values from -0.0625 to 0.0625
Outputs:
- solved_first: float32 [256, 16384], P('col', 'leaf')
- solved_second: float32 [256, 16384], P('col', 'leaf')
- solved_third: float32 [256, 16384], P('col', 'leaf')
- root_solution: float32 [256, 2, 8192], P('col', None, 'leaf')
Inputs may be any that keep to these rules, and one draw needn't show every extreme that they name: `links_first`: each row names 3 different skeleton blocks of its front. `links_second`: each row names 3 different skeleton blocks of its front. `links_third`: each row names 3 different skeleton blocks of its front. `order_first`: each row is a permutation. `order_second`: each row is a permutation. `order_third`: each row is a permutation.
All inputs are finite; a program needn't handle non-finite values.
Results may differ from a plain program's by a relative error of at most 0.0003.
Values sent between devices are 32-bit elements; how exact they have to be, the bound alone decides.
A program may use at most 64 MiB of HBM per device.

v0:
```python
import jax
import jax.numpy as jnp
from jax import lax
from jax.sharding import PartitionSpec as P


def partner(block, axis, stride):
    count = lax.axis_size(axis)
    route = []
    for low in range(count):
        high = low | 1 << stride
        if high != low and high < count:
            route += [(low, high), (high, low)]
    return lax.ppermute(block, axis, route)


def eliminate(section, inverse, coupling, link_ids, live_count):
    block_rows = inverse.shape[-1]
    red_blocks = inverse.shape[0]
    link_total = coupling.shape[1]
    rhs_rows = section.shape[0]
    skeleton_count = section.shape[1] // block_rows - red_blocks
    redundant = section[:, : red_blocks * block_rows].reshape(rhs_rows, red_blocks, block_rows)
    positions = lax.broadcasted_iota(
        jnp.int32, (red_blocks, block_rows), 0
    ) * block_rows + lax.broadcasted_iota(jnp.int32, (red_blocks, block_rows), 1)
    live_rows = (positions < live_count).astype(jnp.float32)
    solved = (
        jnp.einsum("rib,iba->ria", redundant * live_rows, inverse, precision=lax.Precision.HIGHEST)
        * live_rows
    )
    pushed = jnp.einsum("ria,ikab->rikb", solved, coupling, precision=lax.Precision.HIGHEST)
    targets = (
        link_ids[:, :, None]
        == lax.broadcasted_iota(jnp.int32, (red_blocks, link_total, skeleton_count), 2)
    ).astype(jnp.float32)
    update = jnp.einsum("rikb,iks->rsb", pushed, targets, precision=lax.Precision.HIGHEST)
    skeleton = (
        section[:, red_blocks * block_rows :].reshape(rhs_rows, skeleton_count, block_rows) - update
    )
    return (solved.reshape(rhs_rows, red_blocks * block_rows), skeleton)


def join_halves(skeleton, level_index):
    half_blocks = skeleton.shape[1] // 2
    upper_half = lax.axis_index("leaf") >> level_index & 1
    kept_half = lax.dynamic_slice_in_dim(skeleton, upper_half * half_blocks, half_blocks, 1)
    sent_half = lax.dynamic_slice_in_dim(skeleton, (1 - upper_half) * half_blocks, half_blocks, 1)
    received = partner(sent_half, "leaf", level_index)
    return jnp.where(
        upper_half == 0,
        jnp.concatenate([kept_half, received], 1),
        jnp.concatenate([received, kept_half], 1),
    )


def spread_columns(values):
    return lax.all_gather(values, "col", axis=0, tiled=True)


def spread_leaf(values):
    return lax.all_gather(values, "leaf", axis=0, tiled=True)


def to_leaf_rows(values):
    full_rows = lax.all_gather(values, "col", axis=1, tiled=True)
    return lax.all_to_all(full_rows, "leaf", split_axis=1, concat_axis=0, tiled=True)


def to_column_rows(values):
    full_rows = lax.all_gather(values, "leaf", axis=1, tiled=True)
    return lax.all_to_all(full_rows, "col", split_axis=1, concat_axis=0, tiled=True)


def forward_product(values, matrix):
    return lax.psum_scatter(
        jnp.dot(
            values, matrix, precision=lax.Precision.HIGHEST, preferred_element_type=jnp.float32
        ),
        "leaf",
        scatter_dimension=0,
        tiled=True,
    )


def backward_product(values, matrix):
    return lax.psum_scatter(
        lax.dot_general(
            values,
            matrix,
            (((1,), (1,)), ((), ())),
            precision=lax.Precision.HIGHEST,
            preferred_element_type=jnp.float32,
        ),
        "col",
        scatter_dimension=0,
        tiled=True,
    )


def local(
    right_sides,
    inverse_first,
    coupling_first,
    links_first,
    order_first,
    inverse_second,
    coupling_second,
    links_second,
    order_second,
    inverse_third,
    coupling_third,
    links_third,
    order_third,
    front_rows,
    root_inverse,
    root_coupling,
):
    level_data = (
        (inverse_first, coupling_first, links_first, order_first),
        (inverse_second, coupling_second, links_second, order_second),
        (inverse_third, coupling_third, links_third, order_third),
    )
    section = right_sides
    outputs = []
    for level_index in range(3):
        inverse, coupling, link_ids, order_map = level_data[level_index]
        solved, skeleton = eliminate(
            section, inverse, coupling, link_ids, front_rows[level_index, 0]
        )
        outputs.append(solved)
        if level_index < 2:
            skeleton = join_halves(skeleton, level_index)
        skeleton = jnp.take(skeleton, order_map[0], axis=1)
        section = skeleton.reshape(skeleton.shape[0], -1)
    rhs_rows = right_sides.shape[0]
    panel_count = root_inverse.shape[0]
    panel_rows = root_inverse.shape[1]
    root_rhs = section.reshape(rhs_rows, panel_count, panel_rows)
    full_rhs = spread_columns(root_rhs)
    first_solve = forward_product(full_rhs[:, 0], root_inverse[0])
    coupled = forward_product(to_leaf_rows(first_solve), root_coupling)
    second_solve = forward_product(full_rhs[:, 1] - to_leaf_rows(coupled), root_inverse[1])
    forward_both = spread_leaf(jnp.stack([first_solve, second_solve], 1))
    last_panel = backward_product(forward_both[:, 1], root_inverse[1])
    back_coupled = backward_product(to_column_rows(last_panel), root_coupling)
    first_panel = backward_product(
        forward_both[:, 0] - to_column_rows(back_coupled), root_inverse[0]
    )
    root_solution = jnp.stack([first_panel, last_panel], 1)
    return (outputs[0], outputs[1], outputs[2], root_solution)


def solution(mesh):
    in_specs = (
        P("col", "leaf"),
        P("leaf", None, None),
        P("leaf", None, None, None),
        P("leaf", None),
        P("leaf", None),
        P("leaf", None, None),
        P("leaf", None, None, None),
        P("leaf", None),
        P("leaf", None),
        P("leaf", None, None),
        P("leaf", None, None, None),
        P("leaf", None),
        P("leaf", None),
        P(None, "leaf"),
        P(None, "leaf", "col"),
        P("leaf", "col"),
    )
    out_specs = (P("col", "leaf"), P("col", "leaf"), P("col", "leaf"), P("col", None, "leaf"))
    return jax.shard_map(local, mesh=mesh, in_specs=in_specs, out_specs=out_specs, check_vma=False)
```

profile of v0, /device:TPU:2, one launch (start us, length us, event | category | flops | bytes accessed | tf_op | source)
XLA Modules:
  0.0 1212.6 jit_solution(16037484874511490501)
XLA Ops:
  8.6 0.9 slice-done
  9.6 2.0 fusion.47
  11.6 1.3 convolution_multiply_fusion.2
  13.9 1.9 collective-permute-start
  20.2 0.8 copy-done.7
  22.4 3.8 collective-permute-start.1
  26.3 1.9 collective-permute-done.1
  29.0 0.8 copy-done.8
  31.6 62.8 %all_gather.18 = f32[256,2,256]{2,1,0:T(2,128)S(1)} all-gather(f32[16,2,256]{2,1,0:T(2,128)S(1)} %broadcast_select_fusion), channel_id=1, replica_groups=mesh['leaf'=32,'col'=16] {'col'}, dimensions={0}, use_global_device_ids=true | all-gather | bytes 557056 | tf_op jit(solution)/shard_map/all_gather | solution.py:58
  94.7 1.4 fusion.11
  96.2 123.1 %reduce-scatter.7.cloned.1.call-done = f32[8,512]{1,0:T(8,128)} async-done(((f32[256,512]{1,0:T(8,128)}), f32[8,512]{1,0:T(8,128)}) %reduce-scatter.7.cloned.1.call-update) | async-done | bytes 16400 | tf_op jit(solution)/shard_map/reduce_scatter | solution.py:76
  219.2 53.1 %all_gather.19 = f32[8,8192]{1,0:T(8,128)S(1)} all-gather(f32[8,512]{1,0:T(8,128)} %reduce-scatter.7.cloned.1.call-done), channel_id=1, replica_groups=mesh['leaf'=32,'col'=16] {'col'}, dimensions={1}, use_global_device_ids=true | all-gather | bytes 278528 | tf_op jit(solution)/shard_map/all_gather | solution.py:66
  272.4 32.4 %all_to_all.76 = f32[8,32,256]{2,0,1:T(8,128)S(1)} all-to-all(f32[8,32,256]{2,0,1:T(8,128)S(1)} %bitcast.194), channel_id=1, replica_groups=mesh['leaf'=32,'col'=16] {'leaf'}, dimensions={1} | all-to-all | bytes 524288 | tf_op jit(solution)/shard_map/all_to_all | solution.py:67
  304.8 1.4 fusion.21
  306.3 121.1 %reduce-scatter.9.cloned.1.call-done = f32[8,512]{1,0:T(8,128)} async-done(((f32[256,512]{1,0:T(8,128)}), f32[8,512]{1,0:T(8,128)}) %reduce-scatter.9.cloned.1.call-update) | async-done | bytes 16400 | tf_op jit(solution)/shard_map/reduce_scatter | solution.py:76
  427.4 52.9 %all_gather.20 = f32[8,8192]{1,0:T(8,128)S(1)} all-gather(f32[8,512]{1,0:T(8,128)} %reduce-scatter.9.cloned.1.call-done), channel_id=1, replica_groups=mesh['leaf'=32,'col'=16] {'col'}, dimensions={1}, use_global_device_ids=true | all-gather | bytes 278528 | tf_op jit(solution)/shard_map/all_gather | solution.py:66
  480.3 32.5 %all_to_all.77 = f32[8,32,256]{2,0,1:T(8,128)S(1)} all-to-all(f32[8,32,256]{2,0,1:T(8,128)S(1)} %bitcast.192), channel_id=1, replica_groups=mesh['leaf'=32,'col'=16] {'leaf'}, dimensions={1} | all-to-all | bytes 524288 | tf_op jit(solution)/shard_map/all_to_all | solution.py:67
  513.4 1.4 fusion.8
  514.9 121.2 %reduce-scatter.11.cloned.1.call-done = f32[8,512]{1,0:T(8,128)} async-done(((f32[256,512]{1,0:T(8,128)}), f32[8,512]{1,0:T(8,128)}) %reduce-scatter.11.cloned.1.call-update) | async-done | bytes 16400 | tf_op jit(solution)/shard_map/reduce_scatter | solution.py:76
  636.1 1.3 pad_maximum_fusion
  637.5 81.3 %all-gather.2.cloned.1.call-done = f32[256,2,512]{2,0,1:T(8,128)} async-done(((f32[8,2,512]{2,0,1:T(8,128)}), f32[256,2,512]{2,0,1:T(8,128)}) %all-gather.2.cloned.1.call-update) | async-done | bytes 1048592 | tf_op jit(solution)/shard_map/all_gather | solution.py:62
  718.8 2.4 fusion.3
  721.3 113.1 %reduce-scatter.13.cloned.1.call-done = f32[16,256]{1,0:T(8,128)} async-done(((f32[256,256]{1,0:T(8,128)}), f32[16,256]{1,0:T(8,128)}) %reduce-scatter.13.cloned.1.call-update) | async-done | bytes 16400 | tf_op jit(solution)/shard_map/reduce_scatter | solution.py:87
  834.3 36.0 %all_gather.22 = f32[16,8192]{1,0:T(8,128)S(1)} all-gather(f32[16,256]{1,0:T(8,128)} %reduce-scatter.13.cloned.1.call-done), channel_id=1, replica_groups=mesh['leaf'=32,'col'=16] {'leaf'}, dimensions={1}, use_global_device_ids=true | all-gather | bytes 540672 | tf_op jit(solution)/shard_map/all_gather | solution.py:71
  870.4 41.3 %all_to_all.78 = f32[16,16,512]{2,0,1:T(8,128)S(1)} all-to-all(f32[16,16,512]{2,0,1:T(8,128)S(1)} %bitcast.187), channel_id=1, replica_groups=mesh['leaf'=32,'col'=16] {'col'}, dimensions={1} | all-to-all | bytes 1048576 | tf_op jit(solution)/shard_map/all_to_all | solution.py:72
  911.7 1.3 fusion.53
  913.1 106.2 %reduce-scatter.15.cloned.1.call-done = f32[16,256]{1,0:T(8,128)} async-done(((f32[256,256]{1,0:T(8,128)}), f32[16,256]{1,0:T(8,128)}) %reduce-scatter.15.cloned.1.call-update) | async-done | bytes 16400 | tf_op jit(solution)/shard_map/reduce_scatter | solution.py:87
  1019.3 36.1 %all_gather.23 = f32[16,8192]{1,0:T(8,128)S(1)} all-gather(f32[16,256]{1,0:T(8,128)} %reduce-scatter.15.cloned.1.call-done), channel_id=1, replica_groups=mesh['leaf'=32,'col'=16] {'leaf'}, dimensions={1}, use_global_device_ids=true | all-gather | bytes 540672 | tf_op jit(solution)/shard_map/all_gather | solution.py:71
  1055.4 41.4 %all_to_all.79 = f32[16,16,512]{2,0,1:T(8,128)S(1)} all-to-all(f32[16,16,512]{2,0,1:T(8,128)S(1)} %bitcast.190), channel_id=1, replica_groups=mesh['leaf'=32,'col'=16] {'col'}, dimensions={1} | all-to-all | bytes 1048576 | tf_op jit(solution)/shard_map/all_to_all | solution.py:72
  1096.8 1.3 fusion.5
  1099.4 105.0 %reduce-scatter.17.cloned.1.call-done = f32[16,256]{1,0:T(8,128)} async-done(((f32[256,256]{1,0:T(8,128)}), f32[16,256]{1,0:T(8,128)}) %reduce-scatter.17.cloned.1.call-update) | async-done | bytes 16400 | tf_op jit(solution)/shard_map/reduce_scatter | solution.py:87
  1204.4 0.7 pad_maximum_fusion.1
  (114 shorter events, 13.7 us)
Async XLA Ops:
  7.2 5.7 copy-start
  7.2 212.1 %reduce-scatter.7.cloned.1.call-start = ((), (), s32[]{:S(2)}) async-start(), calls=%async_computation.10 | async-start | bytes 540672 | tf_op jit(solution)/shard_map/reduce_scatter | solution.py:76
  7.2 0.7 copy-start.11
  7.2 1.3 copy-start.12
  8.6 0.9 slice-start
  9.5 2.1 copy-start.6
  13.9 1.9 copy-start.15
  13.9 5.6 collective-permute-start
  15.8 0.7 copy-start.16
  16.5 0.7 copy-start.17
  18.7 0.7 copy-start.13
  19.5 1.9 copy-start.4
  20.1 1.0 copy-start.7
  21.4 4.8 copy-start.14
  22.0 8.1 copy-start.5
  22.4 5.9 collective-permute-start.1
  28.8 1.0 copy-start.8
  30.1 64.5 %copy-start.1 = (f32[2,256,512]{2,1,0:T(8,128)S(1)}, f32[2,256,512]{2,1,0:T(8,128)}, u32[]{:S(2)}) copy-start(f32[2,256,512]{2,1,0:T(8,128)} %param.30) | copy-start | bytes 3145732
  96.1 208.7 %copy-start.2 = (f32[256,512]{1,0:T(8,128)S(1)}, f32[256,512]{1,0:T(8,128)}, u32[]{:S(2)}) copy-start(f32[256,512]{1,0:T(8,128)} %param.31) | copy-start | bytes 1572868
  96.1 331.2 %reduce-scatter.9.cloned.1.call-start = ((), (), s32[]{:S(2)}) async-start(), calls=%async_computation.11 | async-start | bytes 540672 | tf_op jit(solution)/shard_map/reduce_scatter | solution.py:76
  306.3 329.9 %reduce-scatter.11.cloned.1.call-start = ((), (), s32[]{:S(2)}) async-start(), calls=%async_computation.12 | async-start | bytes 540672 | tf_op jit(solution)/shard_map/reduce_scatter | solution.py:76
  514.8 121.3 %copy-start.10 = (f32[8,512]{1,0:T(8,128)S(1)}, f32[8,512]{1,0:T(8,128)}, u32[]{:S(2)}) copy-start(f32[8,512]{1,0:T(8,128)} %reduce-scatter.7.cloned.1.call-done) | copy-start | bytes 49156
  514.9 204.0 %all-gather.2.cloned.1.call-start = ((), (), s32[]{:S(2)}) async-start(), calls=%async_computation.13 | async-start | bytes 1081344 | tf_op jit(solution)/shard_map/all_gather | solution.py:62
  637.5 196.9 %reduce-scatter.13.cloned.1.call-start = ((), (), s32[]{:S(2)}) async-start(), calls=%async_computation.14 | async-start | bytes 278528 | tf_op jit(solution)/shard_map/reduce_scatter | solution.py:87
  721.2 298.1 %reduce-scatter.15.cloned.1.call-start = ((), (), s32[]{:S(2)}) async-start(), calls=%async_computation.15 | async-start | bytes 278528 | tf_op jit(solution)/shard_map/reduce_scatter | solution.py:87
  913.0 291.4 %reduce-scatter.17.cloned.1.call-start = ((), (), s32[]{:S(2)}) async-start(), calls=%async_computation.16 | async-start | bytes 278528 | tf_op jit(solution)/shard_map/reduce_scatter | solution.py:87
  1055.4 41.4 %copy-start.3 = (f32[256,2,512]{2,0,1:T(8,128)S(1)}, f32[256,2,512]{2,0,1:T(8,128)}, u32[]{:S(2)}) copy-start(f32[256,2,512]{2,0,1:T(8,128)} %all-gather.2.cloned.1.call-done) | copy-start | bytes 3145732
  1098.8 105.6 %copy-start.9 = (f32[16,256]{1,0:T(8,128)S(1)}, f32[16,256]{1,0:T(8,128)}, u32[]{:S(2)}) copy-start(f32[16,256]{1,0:T(8,128)} %reduce-scatter.13.cloned.1.call-done) | copy-start | bytes 49156
Sparse Core Ops, SparseCore 0:
  96.2 122.9 reduce-scatter.6
  306.4 120.9 reduce-scatter.8
  515.0 121.0 reduce-scatter.10
  638.9 79.8 all-gather.1
  723.2 111.0 reduce-scatter.12
  913.2 106.0 reduce-scatter.14
  1098.3 106.0 reduce-scatter.16
where the time goes:
time: 1210 us
  waiting for transfers between devices  773 us (64%)
  blocking collectives  389 us (32%)
  between operations  14.6 us (1%)
  matrix products  13.9 us (1%)
    reduce_scatter x3, waiting for transfers between devices, forward_product(): lax.psum_scatter(jnp.dot(values, matrix, precision=lax.Precision.HIGHEST,...  365 us
    reduce_scatter x3, waiting for transfers between devices, backward_product(): lax.psum_scatter(lax.dot_general(values, matrix, (((1,), (1,)), ((), ()))...  324 us
    all_gather x2, blocking collectives, to_leaf_rows(): full_rows = lax.all_gather(values, 'col', axis=1, tiled=True)  106 us
    all_to_all x2, blocking collectives, to_column_rows(): lax.all_to_all(full_rows, 'col', split_axis=1, concat_axis=0, tiled=True)  82.7 us
    all_gather x1, waiting for transfers between devices, spread_leaf(): return lax.all_gather(values, 'leaf', axis=0, tiled=True)  81.3 us
    all_gather x2, blocking collectives, to_column_rows(): full_rows = lax.all_gather(values, 'leaf', axis=1, tiled=True)  72.1 us
    all_to_all x2, blocking collectives, to_leaf_rows(): lax.all_to_all(full_rows, 'leaf', split_axis=1, concat_axis=0, tiled=True)  64.9 us
    all_gather x1, blocking collectives, spread_columns(): return lax.all_gather(values, 'col', axis=0, tiled=True)  62.8 us
  transfers between devices with their start and end apart: 9, of which 8 were waited for; matrix products, arithmetic and copies ran while one was open for 0% of the time, Pallas kernels for 0%

commit v1 on v0

--- a/solution.py
+++ b/solution.py
@@ -2,6 +2,15 @@
 import jax.numpy as jnp
 from jax import lax
 from jax.sharding import PartitionSpec as P
+
+
+def tracks_store(device_axis, s0):
+    return jnp.concatenate(
+        lax.all_to_all(
+            jnp.stack(jnp.split(s0, lax.axis_size(device_axis), axis=1)), device_axis, 0, 0
+        ),
+        axis=0,
+    )
 
 
 def partner(block, axis, stride):
@@ -69,7 +78,7 @@
 
 def to_column_rows(values):
     full_rows = lax.all_gather(values, "leaf", axis=1, tiled=True)
-    return lax.all_to_all(full_rows, "col", split_axis=1, concat_axis=0, tiled=True)
+    return tracks_store("col", full_rows)
 
 
 def forward_product(values, matrix):

time: 1210 us -> 1210 us (level)
  no operation moved by 1% of the time
where the time goes in v1:
time: 1210 us
  waiting for transfers between devices  773 us (64%)
  blocking collectives  389 us (32%)
  between operations  14.8 us (1%)
  matrix products  13.9 us (1%)
    reduce_scatter x3, waiting for transfers between devices, forward_product(): lax.psum_scatter(jnp.dot(values, matrix, precision=lax.Precision.HIGHEST,...  365 us
    reduce_scatter x3, waiting for transfers between devices, backward_product(): lax.psum_scatter(lax.dot_general(values, matrix, (((1,), (1,)), ((), ()))...  324 us
    all_gather x2, blocking collectives, to_leaf_rows(): full_rows = lax.all_gather(values, 'col', axis=1, tiled=True)  106 us
    all_to_all x2, blocking collectives, tracks_store(): lax.all_to_all(jnp.stack(jnp.split(s0, lax.axis_size(device_axis), axis=1...  82.7 us
    all_gather x1, waiting for transfers between devices, spread_leaf(): return lax.all_gather(values, 'leaf', axis=0, tiled=True)  81.3 us
    all_gather x2, blocking collectives, to_column_rows(): full_rows = lax.all_gather(values, 'leaf', axis=1, tiled=True)  72.1 us
    all_to_all x2, blocking collectives, to_leaf_rows(): lax.all_to_all(full_rows, 'leaf', split_axis=1, concat_axis=0, tiled=True)  64.9 us
    all_gather x1, blocking collectives, spread_columns(): return lax.all_gather(values, 'col', axis=0, tiled=True)  62.8 us
  transfers between devices with their start and end apart: 9, of which 8 were waited for; matrix products, arithmetic and copies ran while one was open for 0% of the time, Pallas kernels for 0%

profile of v1, /device:TPU:2, one launch (start us, length us, event | category | flops | bytes accessed | tf_op | source)
XLA Modules:
  0.0 1212.9 jit_solution(6717064641563398963)
XLA Ops:
  8.6 0.9 slice-done
  9.6 2.0 fusion.47
  11.6 1.3 convolution_multiply_fusion.2
  13.9 1.9 collective-permute-start
  20.2 0.8 copy-done.7
  22.4 3.8 collective-permute-start.1
  26.3 1.9 collective-permute-done.1
  29.0 0.8 copy-done.8
  31.6 62.8 %all_gather.18 = f32[256,2,256]{2,1,0:T(2,128)S(1)} all-gather(f32[16,2,256]{2,1,0:T(2,128)S(1)} %broadcast_select_fusion), channel_id=1, replica_groups=mesh['leaf'=32,'col'=16] {'col'}, dimensions={0}, use_global_device_ids=true | all-gather | bytes 557056 | tf_op jit(solution)/shard_map/all_gather | solution.py:67
  94.7 1.4 fusion.11
  96.2 123.1 %reduce-scatter.7.cloned.1.call-done = f32[8,512]{1,0:T(8,128)} async-done(((f32[256,512]{1,0:T(8,128)}), f32[8,512]{1,0:T(8,128)}) %reduce-scatter.7.cloned.1.call-update) | async-done | bytes 16400 | tf_op jit(solution)/shard_map/reduce_scatter | solution.py:85
  219.2 53.1 %all_gather.19 = f32[8,8192]{1,0:T(8,128)S(1)} all-gather(f32[8,512]{1,0:T(8,128)} %reduce-scatter.7.cloned.1.call-done), channel_id=1, replica_groups=mesh['leaf'=32,'col'=16] {'col'}, dimensions={1}, use_global_device_ids=true | all-gather | bytes 278528 | tf_op jit(solution)/shard_map/all_gather | solution.py:75
  272.4 32.4 %all_to_all.48 = f32[8,32,256]{2,0,1:T(8,128)S(1)} all-to-all(f32[8,32,256]{2,0,1:T(8,128)S(1)} %bitcast.306), channel_id=1, replica_groups=mesh['leaf'=32,'col'=16] {'leaf'}, dimensions={1} | all-to-all | bytes 524288 | tf_op jit(solution)/shard_map/all_to_all | solution.py:76
  304.8 1.4 fusion.21
  306.3 121.1 %reduce-scatter.9.cloned.1.call-done = f32[8,512]{1,0:T(8,128)} async-done(((f32[256,512]{1,0:T(8,128)}), f32[8,512]{1,0:T(8,128)}) %reduce-scatter.9.cloned.1.call-update) | async-done | bytes 16400 | tf_op jit(solution)/shard_map/reduce_scatter | solution.py:85
  427.4 52.9 %all_gather.20 = f32[8,8192]{1,0:T(8,128)S(1)} all-gather(f32[8,512]{1,0:T(8,128)} %reduce-scatter.9.cloned.1.call-done), channel_id=1, replica_groups=mesh['leaf'=32,'col'=16] {'col'}, dimensions={1}, use_global_device_ids=true | all-gather | bytes 278528 | tf_op jit(solution)/shard_map/all_gather | solution.py:75
  480.3 32.5 %all_to_all.49 = f32[8,32,256]{2,0,1:T(8,128)S(1)} all-to-all(f32[8,32,256]{2,0,1:T(8,128)S(1)} %bitcast.304), channel_id=1, replica_groups=mesh['leaf'=32,'col'=16] {'leaf'}, dimensions={1} | all-to-all | bytes 524288 | tf_op jit(solution)/shard_map/all_to_all | solution.py:76
  513.4 1.4 fusion.8
  514.9 121.2 %reduce-scatter.11.cloned.1.call-done = f32[8,512]{1,0:T(8,128)} async-done(((f32[256,512]{1,0:T(8,128)}), f32[8,512]{1,0:T(8,128)}) %reduce-scatter.11.cloned.1.call-update) | async-done | bytes 16400 | tf_op jit(solution)/shard_map/reduce_scatter | solution.py:85
  636.1 1.3 pad_maximum_fusion
  637.5 81.3 %all-gather.2.cloned.1.call-done = f32[256,2,512]{2,0,1:T(8,128)} async-done(((f32[8,2,512]{2,0,1:T(8,128)}), f32[256,2,512]{2,0,1:T(8,128)}) %all-gather.2.cloned.1.call-update) | async-done | bytes 1048592 | tf_op jit(solution)/shard_map/all_gather | solution.py:71
  718.8 2.4 fusion.3
  721.3 113.1 %reduce-scatter.13.cloned.1.call-done = f32[16,256]{1,0:T(8,128)} async-done(((f32[256,256]{1,0:T(8,128)}), f32[16,256]{1,0:T(8,128)}) %reduce-scatter.13.cloned.1.call-update) | async-done | bytes 16400 | tf_op jit(solution)/shard_map/reduce_scatter | solution.py:96
  834.3 36.0 %all_gather.22 = f32[16,8192]{1,0:T(8,128)S(1)} all-gather(f32[16,256]{1,0:T(8,128)} %reduce-scatter.13.cloned.1.call-done), channel_id=1, replica_groups=mesh['leaf'=32,'col'=16] {'leaf'}, dimensions={1}, use_global_device_ids=true | all-gather | bytes 540672 | tf_op jit(solution)/shard_map/all_gather | solution.py:80
  870.6 41.3 %all_to_all.50 = f32[16,16,512]{2,1,0:T(8,128)S(1)} all-to-all(f32[16,16,512]{2,1,0:T(8,128)S(1)} %constant_dynamic-update-slice_fusion), channel_id=1, replica_groups=mesh['leaf'=32,'col'=16] {'col'}, dimensions={0} | all-to-all | bytes 1048576 | tf_op jit(solution)/shard_map/all_to_all | solution.py:9
  911.8 1.3 fusion.53
  913.2 106.2 %reduce-scatter.15.cloned.1.call-done = f32[16,256]{1,0:T(8,128)} async-done(((f32[256,256]{1,0:T(8,128)}), f32[16,256]{1,0:T(8,128)}) %reduce-scatter.15.cloned.1.call-update) | async-done | bytes 16400 | tf_op jit(solution)/shard_map/reduce_scatter | solution.py:96
  1019.4 36.1 %all_gather.23 = f32[16,8192]{1,0:T(8,128)S(1)} all-gather(f32[16,256]{1,0:T(8,128)} %reduce-scatter.15.cloned.1.call-done), channel_id=1, replica_groups=mesh['leaf'=32,'col'=16] {'leaf'}, dimensions={1}, use_global_device_ids=true | all-gather | bytes 540672 | tf_op jit(solution)/shard_map/all_gather | solution.py:80
  1055.7 41.4 %all_to_all.51 = f32[16,16,512]{2,1,0:T(8,128)S(1)} all-to-all(f32[16,16,512]{2,1,0:T(8,128)S(1)} %constant_dynamic-update-slice_fusion.16), channel_id=1, replica_groups=mesh['leaf'=32,'col'=16] {'col'}, dimensions={0} | all-to-all | bytes 1048576 | tf_op jit(solution)/shard_map/all_to_all | solution.py:9
  1097.1 1.3 fusion.5
  1099.7 105.0 %reduce-scatter.17.cloned.1.call-done = f32[16,256]{1,0:T(8,128)} async-done(((f32[256,256]{1,0:T(8,128)}), f32[16,256]{1,0:T(8,128)}) %reduce-scatter.17.cloned.1.call-update) | async-done | bytes 16400 | tf_op jit(solution)/shard_map/reduce_scatter | solution.py:96
  1204.7 0.7 pad_maximum_fusion.1
  (144 shorter events, 13.8 us)
Async XLA Ops:
  7.2 5.7 copy-start
  7.2 212.1 %reduce-scatter.7.cloned.1.call-start = ((), (), s32[]{:S(2)}) async-start(), calls=%async_computation.10 | async-start | bytes 540672 | tf_op jit(solution)/shard_map/reduce_scatter | solution.py:85
  7.2 0.7 copy-start.11
  7.2 1.3 copy-start.12
  8.6 0.9 slice-start
  9.5 2.1 copy-start.6
  13.9 1.9 copy-start.15
  13.9 5.6 collective-permute-start
  15.8 0.7 copy-start.16
  16.5 0.7 copy-start.17
  18.7 0.7 copy-start.13
  19.5 1.9 copy-start.4
  20.1 1.0 copy-start.7
  21.4 4.8 copy-start.14
  22.0 8.1 copy-start.5
  22.4 5.9 collective-permute-start.1
  28.8 1.0 copy-start.8
  30.1 64.5 %copy-start.1 = (f32[2,256,512]{2,1,0:T(8,128)S(1)}, f32[2,256,512]{2,1,0:T(8,128)}, u32[]{:S(2)}) copy-start(f32[2,256,512]{2,1,0:T(8,128)} %param.30) | copy-start | bytes 3145732
  96.1 208.7 %copy-start.2 = (f32[256,512]{1,0:T(8,128)S(1)}, f32[256,512]{1,0:T(8,128)}, u32[]{:S(2)}) copy-start(f32[256,512]{1,0:T(8,128)} %param.31) | copy-start | bytes 1572868
  96.1 331.2 %reduce-scatter.9.cloned.1.call-start = ((), (), s32[]{:S(2)}) async-start(), calls=%async_computation.11 | async-start | bytes 540672 | tf_op jit(solution)/shard_map/reduce_scatter | solution.py:85
  306.3 329.9 %reduce-scatter.11.cloned.1.call-start = ((), (), s32[]{:S(2)}) async-start(), calls=%async_computation.12 | async-start | bytes 540672 | tf_op jit(solution)/shard_map/reduce_scatter | solution.py:85
  514.8 121.3 %copy-start.10 = (f32[8,512]{1,0:T(8,128)S(1)}, f32[8,512]{1,0:T(8,128)}, u32[]{:S(2)}) copy-start(f32[8,512]{1,0:T(8,128)} %reduce-scatter.7.cloned.1.call-done) | copy-start | bytes 49156
  514.9 204.0 %all-gather.2.cloned.1.call-start = ((), (), s32[]{:S(2)}) async-start(), calls=%async_computation.13 | async-start | bytes 1081344 | tf_op jit(solution)/shard_map/all_gather | solution.py:71
  637.5 196.9 %reduce-scatter.13.cloned.1.call-start = ((), (), s32[]{:S(2)}) async-start(), calls=%async_computation.14 | async-start | bytes 278528 | tf_op jit(solution)/shard_map/reduce_scatter | solution.py:96
  721.2 298.2 %reduce-scatter.15.cloned.1.call-start = ((), (), s32[]{:S(2)}) async-start(), calls=%async_computation.15 | async-start | bytes 278528 | tf_op jit(solution)/shard_map/reduce_scatter | solution.py:96
  913.2 291.5 %reduce-scatter.17.cloned.1.call-start = ((), (), s32[]{:S(2)}) async-start(), calls=%async_computation.16 | async-start | bytes 278528 | tf_op jit(solution)/shard_map/reduce_scatter | solution.py:96
  1055.5 41.6 %copy-start.3 = (f32[256,2,512]{2,0,1:T(8,128)S(1)}, f32[256,2,512]{2,0,1:T(8,128)}, u32[]{:S(2)}) copy-start(f32[256,2,512]{2,0,1:T(8,128)} %all-gather.2.cloned.1.call-done) | copy-start | bytes 3145732
  1099.1 105.6 %copy-start.9 = (f32[16,256]{1,0:T(8,128)S(1)}, f32[16,256]{1,0:T(8,128)}, u32[]{:S(2)}) copy-start(f32[16,256]{1,0:T(8,128)} %reduce-scatter.13.cloned.1.call-done) | copy-start | bytes 49156
Sparse Core Ops, SparseCore 0:
  96.2 122.9 reduce-scatter.6
  306.4 120.9 reduce-scatter.8
  515.0 121.0 reduce-scatter.10
  638.9 79.8 all-gather.1
  723.2 111.0 reduce-scatter.12
  913.3 106.0 reduce-scatter.14
  1098.6 106.0 reduce-scatter.16
